TPU v7x, 32 devices: a whole 2x2x4 slice. The times are simulated.
32 devices in a mesh: ctx: 8 (over y, x, core), wt: 4 (over z).
Axes of the slice: x: 2, y: 2, z: 4, core: 2. Of those that a mesh axis runs over, the one named last changes fastest.
Arguments:
- words: bfloat16 [6144, 512], P(('ctx', 'wt')), may hold values from -6 to 6
- teacher: bfloat16 [6144, 512], P(('ctx', 'wt')), may hold values from -6 to 6
- valid: int32 [6144], P(('ctx', 'wt')), may hold values from 0 to 1, as said below
- lengths: int32 [4], replicated, may hold values from 384 to 3072, as said below
- deal: int32 [32], replicated, may hold values from 0 to 31, as said below
- gain_attn: bfloat16 [512], P('wt'), may hold values from 0.25 to 1.75
- shift_attn: bfloat16 [512], P('wt'), may hold values from -3 to 3
- w_qkv: bfloat16 [512, 1536], P('wt'), may hold values from -0.25 to 0.25
- w_out: bfloat16 [512, 512], P('wt'), may hold values from -2 to 2
- gain_mlp: bfloat16 [512], P('wt'), may hold values from 0.25 to 1.75
- shift_mlp: bfloat16 [512], P('wt'), may hold values from -3 to 3
- w_up: bfloat16 [512, 2048], P('wt'), may hold values from -0.25 to 0.25
- w_down: bfloat16 [2048, 512], P('wt'), may hold values from -0.125 to 0.125
Outputs:
- layer_out: bfloat16 [6144, 512], P(('ctx', 'wt'))
- loss: float32 [], replicated
- grad_words: float32 [6144, 512], P(('ctx', 'wt'))
- grad_gain_attn: float32 [512], P('wt')
- grad_shift_attn: float32 [512], P('wt')
- grad_w_qkv: float32 [512, 1536], P('wt')
- grad_w_out: float32 [512, 512], P('wt')
- grad_gain_mlp: float32 [512], P('wt')
- grad_shift_mlp: float32 [512], P('wt')
- grad_w_up: float32 [512, 2048], P('wt')
- grad_w_down: float32 [2048, 512], P('wt')
Inputs may be any that keep to these rules, and one draw needn't show every extreme that they name: lengths are multiples of 192 that sum to 6144; one sequence has exactly 3072 words. `deal`: each initial block appears once; initial blocks that differ by a multiple of the number of ctx indices lie on the same ctx index. The first word of every dealt block is valid.
All inputs are finite; a program needn't handle non-finite values.
Results may differ from a plain program's by a relative error of at most 0.02.
Values may be sent and summed in bfloat16 or wider, within the bound.
No kernel may reach another device: no remote copies, remote signals or barrier semaphores. Data moves between devices by JAX's collectives and lax.ppermute only.
A program may use at most 128 MiB of HBM per device.

v0:
```python
import jax
import jax.numpy as jnp
from jax import lax
from jax.sharding import PartitionSpec as P

H = 8
HEAD = 64
EPS = 1e-05
LOSS_SCALE = 262144.0


def norm_forward(values, gain_vec, shift_vec):
    center = values - jnp.mean(values, axis=-1, keepdims=True)
    inverse = lax.rsqrt(jnp.mean(center * center, axis=-1, keepdims=True) + EPS)
    unit_rows = center * inverse
    return (unit_rows * gain_vec + shift_vec, unit_rows, inverse)


def norm_backward(upstream, unit_rows, inverse, gain_vec):
    scaled = upstream * gain_vec
    inner_term = jnp.mean(scaled * unit_rows, axis=-1, keepdims=True)
    result = inverse * (scaled - jnp.mean(scaled, axis=-1, keepdims=True) - unit_rows * inner_term)
    return (result, jnp.sum(upstream * unit_rows, axis=0), jnp.sum(upstream, axis=0))


def per_device(
    words,
    teacher,
    valid,
    lengths,
    deal,
    gain_attn,
    shift_attn,
    w_qkv,
    w_out,
    gain_mlp,
    shift_mlp,
    w_up,
    w_down,
):
    ctx_count = lax.axis_size("ctx")
    wt_count = lax.axis_size("wt")
    blk_rows = words.shape[0]
    model_width = words.shape[1]
    head_count = H // wt_count
    col_span = 3 * head_count * HEAD
    group_rows = blk_rows * wt_count
    score_scale = HEAD ** (-0.5)
    qkv_full, out_full, gain_first_raw, shift_first_raw = (
        lax.all_gather(w_qkv, "wt", axis=0, tiled=True),
        lax.all_gather(w_out, "wt", axis=0, tiled=True),
        lax.all_gather(gain_attn, "wt", axis=0, tiled=True),
        lax.all_gather(shift_attn, "wt", axis=0, tiled=True),
    )
    qkv_grouped = qkv_full.reshape(model_width, wt_count, col_span)
    out_grouped = out_full.reshape(wt_count, head_count * HEAD, model_width)
    gain_first = gain_first_raw.astype(jnp.float32)
    shift_first = shift_first_raw.astype(jnp.float32)
    inputs = words.astype(jnp.float32)
    normed_one, unit_first, inverse_first = norm_forward(inputs, gain_first, shift_first)
    packed_first = normed_one.astype(jnp.bfloat16)
    projected = jnp.einsum(
        "rd,dwc->wrc", packed_first, qkv_grouped, preferred_element_type=jnp.float32
    ).astype(jnp.bfloat16)
    head_rows = lax.all_to_all(
        projected.reshape(wt_count, blk_rows * col_span),
        "wt",
        split_axis=0,
        concat_axis=0,
        tiled=True,
    )
    head_rows = head_rows.reshape(group_rows, head_count, 3, HEAD)
    queries = head_rows[:, :, 0]
    own_kv = head_rows[:, :, 1:]
    key_values = own_kv.reshape(group_rows, head_count * 2 * HEAD)
    gathered = lax.all_gather(key_values, "ctx", axis=0, tiled=True).reshape(
        ctx_count, group_rows, head_count, 2, HEAD
    )
    offsets = jnp.arange(blk_rows, dtype=jnp.int32)
    bounds = jnp.cumsum(lengths)
    key_place = (deal[:, None] * blk_rows + offsets[None, :]).reshape(ctx_count, group_rows)
    key_seq = jnp.sum((key_place[:, :, None] >= bounds[None, None, :]).astype(jnp.int32), axis=-1)
    ctx_here = lax.axis_index("ctx")
    query_place = lax.dynamic_index_in_dim(key_place, ctx_here, 0, keepdims=False)
    query_seq = lax.dynamic_index_in_dim(key_seq, ctx_here, 0, keepdims=False)
    live_pieces = jnp.ones((ctx_count,), dtype=bool)
    scan_items = (gathered, key_place, key_seq, live_pieces)

    def scores_of(kv_piece, piece_place, piece_seq):
        raw_scores = (
            jnp.einsum(
                "qhd,khd->hqk", queries, kv_piece[:, :, 0], preferred_element_type=jnp.float32
            )
            * score_scale
        )
        visible = (piece_seq[None, :] == query_seq[:, None]) & (
            piece_place[None, :] <= query_place[:, None]
        )
        return (raw_scores, visible[None])

    def forward_step(carry, item):
        kv_piece, piece_place, piece_seq, live_piece = item
        running_max, running_sum, running_acc = carry
        raw_scores, visible = scores_of(kv_piece, piece_place, piece_seq)
        piece_max = jnp.max(jnp.where(visible, raw_scores, -1e30), axis=-1)
        new_max = jnp.maximum(running_max, piece_max)
        weights = jnp.where(visible, jnp.exp(raw_scores - new_max[..., None]), 0.0)
        factor = jnp.exp(running_max - new_max)
        new_sum = running_sum * factor + jnp.sum(weights, axis=-1)
        new_acc = running_acc * factor.T[:, :, None] + jnp.einsum(
            "hqk,khd->qhd",
            weights.astype(jnp.bfloat16),
            kv_piece[:, :, 1],
            preferred_element_type=jnp.float32,
        )
        return ((new_max, new_sum, new_acc), None)

    start_max = jnp.full((head_count, group_rows), -1e30, jnp.float32)
    start_sum = jnp.zeros((head_count, group_rows), jnp.float32)
    start_acc = jnp.zeros((group_rows, head_count, HEAD), jnp.float32)
    (row_max, row_sum, row_acc), _ = lax.scan(
        forward_step, (start_max, start_sum, start_acc), scan_items
    )
    log_total = row_max + jnp.log(row_sum)
    attended_full = row_acc / row_sum.T[:, :, None]
    attended_heads = attended_full.astype(jnp.bfloat16)
    attended_rows = lax.all_to_all(
        attended_heads.reshape(wt_count, blk_rows * head_count * HEAD),
        "wt",
        split_axis=0,
        concat_axis=0,
        tiled=True,
    ).reshape(wt_count, blk_rows, head_count * HEAD)
    residual_one = inputs + jnp.einsum(
        "wrc,wcd->rd", attended_rows, out_grouped, preferred_element_type=jnp.float32
    )
    up_full, down_full, gain_second_raw, shift_second_raw = (
        lax.all_gather(w_up, "wt", axis=0, tiled=True),
        lax.all_gather(w_down, "wt", axis=0, tiled=True),
        lax.all_gather(gain_mlp, "wt", axis=0, tiled=True),
        lax.all_gather(shift_mlp, "wt", axis=0, tiled=True),
    )
    gain_second = gain_second_raw.astype(jnp.float32)
    shift_second = shift_second_raw.astype(jnp.float32)
    normed_two, unit_second, inverse_second = norm_forward(residual_one, gain_second, shift_second)
    packed_second = normed_two.astype(jnp.bfloat16)
    before_act = jnp.dot(packed_second, up_full, preferred_element_type=jnp.float32)
    activated = jax.nn.gelu(before_act, approximate=False).astype(jnp.bfloat16)
    residual_two = residual_one + jnp.dot(activated, down_full, preferred_element_type=jnp.float32)
    distance = residual_two - teacher.astype(jnp.float32)
    valid_float = valid.astype(jnp.float32)
    count_all, square_all = lax.psum(
        (jnp.sum(valid_float), jnp.sum(valid_float * jnp.sum(distance * distance, axis=-1))),
        ("ctx", "wt"),
    )
    loss_value = square_all / (count_all * model_width)
    grad_two = 2.0 * LOSS_SCALE / (count_all * model_width) * valid_float[:, None] * distance
    grad_branch = grad_two.astype(jnp.bfloat16)
    grad_down = jnp.einsum("rf,rd->fd", activated, grad_branch, preferred_element_type=jnp.float32)
    grad_act = jnp.einsum("rd,fd->rf", grad_branch, down_full, preferred_element_type=jnp.float32)
    _, gelu_back = jax.vjp(lambda hidden_in: jax.nn.gelu(hidden_in, approximate=False), before_act)
    grad_pre = gelu_back(grad_act)[0].astype(jnp.bfloat16)
    grad_up = jnp.einsum("rd,rf->df", packed_second, grad_pre, preferred_element_type=jnp.float32)
    grad_normed_two = jnp.einsum("rf,df->rd", grad_pre, up_full, preferred_element_type=jnp.float32)
    back_two, grad_gain_second, grad_shift_second = norm_backward(
        grad_normed_two, unit_second, inverse_second, gain_second
    )
    grad_one = grad_two + back_two
    grad_attn_out = grad_one.astype(jnp.bfloat16)
    grad_out = jnp.einsum(
        "wrc,rd->wcd", attended_rows, grad_attn_out, preferred_element_type=jnp.float32
    ).reshape(model_width, model_width)
    grad_att_rows = jnp.einsum(
        "rd,wcd->wrc", grad_attn_out, out_grouped, preferred_element_type=jnp.float32
    ).astype(jnp.bfloat16)
    grad_att_heads = lax.all_to_all(
        grad_att_rows.reshape(wt_count, blk_rows * head_count * HEAD),
        "wt",
        split_axis=0,
        concat_axis=0,
        tiled=True,
    ).reshape(group_rows, head_count, HEAD)
    row_delta = jnp.sum(grad_att_heads.astype(jnp.float32) * attended_full, axis=-1).T

    def score_grads(kv_piece, piece_place, piece_seq):
        raw_scores, visible = scores_of(kv_piece, piece_place, piece_seq)
        probs = jnp.where(visible, jnp.exp(raw_scores - log_total[..., None]), 0.0)
        grad_probs = jnp.einsum(
            "qhd,khd->hqk", grad_att_heads, kv_piece[:, :, 1], preferred_element_type=jnp.float32
        )
        return (probs, (probs * (grad_probs - row_delta[..., None])).astype(jnp.bfloat16))

    def grad_step(carry, item):
        kv_piece, piece_place, piece_seq, live_piece = item
        probs, grad_scores = score_grads(kv_piece, piece_place, piece_seq)
        grad_keys = (
            jnp.einsum("hqk,qhd->khd", grad_scores, queries, preferred_element_type=jnp.float32)
            * score_scale
        )
        grad_values = jnp.einsum(
            "hqk,qhd->khd",
            probs.astype(jnp.bfloat16),
            grad_att_heads,
            preferred_element_type=jnp.float32,
        )
        grad_next = carry + jnp.einsum(
            "hqk,khd->qhd", grad_scores, kv_piece[:, :, 0], preferred_element_type=jnp.float32
        )
        return (grad_next, jnp.stack([grad_keys, grad_values], axis=2))

    grad_query_sum, grad_pieces = lax.scan(
        grad_step, jnp.zeros((group_rows, head_count, HEAD), jnp.float32), scan_items
    )
    grad_kv = lax.psum_scatter(
        grad_pieces.reshape(ctx_count * group_rows, head_count * 2 * HEAD).astype(jnp.bfloat16),
        "ctx",
        scatter_dimension=0,
        tiled=True,
    ).astype(jnp.float32)
    grad_kv = grad_kv.astype(jnp.bfloat16).reshape(group_rows, head_count, 2, HEAD)
    grad_queries = (grad_query_sum * score_scale).astype(jnp.bfloat16)
    grad_heads = jnp.concatenate([grad_queries[:, :, None], grad_kv], axis=2)
    grad_rows = lax.all_to_all(
        grad_heads.reshape(wt_count, blk_rows * col_span),
        "wt",
        split_axis=0,
        concat_axis=0,
        tiled=True,
    ).reshape(wt_count, blk_rows, col_span)
    grad_qkv = jnp.einsum(
        "rd,wrc->dwc", packed_first, grad_rows, preferred_element_type=jnp.float32
    ).reshape(model_width, 3 * model_width)
    grad_normed_one = jnp.einsum(
        "wrc,dwc->rd", grad_rows, qkv_grouped, preferred_element_type=jnp.float32
    )
    back_one, grad_gain_first, grad_shift_first = norm_backward(
        grad_normed_one, unit_first, inverse_first, gain_first
    )
    grad_words = grad_one + back_one
    shard_ga, shard_sa, shard_qkv, shard_out, shard_gm, shard_sm, shard_up, shard_down = (
        lax.psum_scatter(
            grad_gain_first.astype(jnp.bfloat16), "wt", scatter_dimension=0, tiled=True
        ).astype(jnp.float32),
        lax.psum_scatter(
            grad_shift_first.astype(jnp.bfloat16), "wt", scatter_dimension=0, tiled=True
        ).astype(jnp.float32),
        lax.psum_scatter(
            grad_qkv.astype(jnp.bfloat16), "wt", scatter_dimension=0, tiled=True
        ).astype(jnp.float32),
        lax.psum_scatter(
            grad_out.astype(jnp.bfloat16), "wt", scatter_dimension=0, tiled=True
        ).astype(jnp.float32),
        lax.psum_scatter(
            grad_gain_second.astype(jnp.bfloat16), "wt", scatter_dimension=0, tiled=True
        ).astype(jnp.float32),
        lax.psum_scatter(
            grad_shift_second.astype(jnp.bfloat16), "wt", scatter_dimension=0, tiled=True
        ).astype(jnp.float32),
        lax.psum_scatter(
            grad_up.astype(jnp.bfloat16), "wt", scatter_dimension=0, tiled=True
        ).astype(jnp.float32),
        lax.psum_scatter(
            grad_down.astype(jnp.bfloat16), "wt", scatter_dimension=0, tiled=True
        ).astype(jnp.float32),
    )
    summed = (
        lax.psum(shard_ga.astype(jnp.bfloat16), "ctx").astype(jnp.float32),
        lax.psum(shard_sa.astype(jnp.bfloat16), "ctx").astype(jnp.float32),
        lax.psum(shard_qkv.astype(jnp.bfloat16), "ctx").astype(jnp.float32),
        lax.psum(shard_out.astype(jnp.bfloat16), "ctx").astype(jnp.float32),
        lax.psum(shard_gm.astype(jnp.bfloat16), "ctx").astype(jnp.float32),
        lax.psum(shard_sm.astype(jnp.bfloat16), "ctx").astype(jnp.float32),
        lax.psum(shard_up.astype(jnp.bfloat16), "ctx").astype(jnp.float32),
        lax.psum(shard_down.astype(jnp.bfloat16), "ctx").astype(jnp.float32),
    )
    return (
        residual_two.astype(jnp.bfloat16),
        loss_value,
        grad_words,
        summed[0],
        summed[1],
        summed[2],
        summed[3],
        summed[4],
        summed[5],
        summed[6],
        summed[7],
    )


def solution(mesh):
    placed = (
        P(("ctx", "wt"), None),
        P(("ctx", "wt"), None),
        P(("ctx", "wt")),
        P(),
        P(),
        P("wt"),
        P("wt"),
        P("wt", None),
        P("wt", None),
        P("wt"),
        P("wt"),
        P("wt", None),
        P("wt", None),
    )
    return jax.shard_map(
        per_device,
        mesh=mesh,
        in_specs=placed,
        out_specs=(
            P(("ctx", "wt"), None),
            P(),
            P(("ctx", "wt"), None),
            P("wt"),
            P("wt"),
            P("wt", None),
            P("wt", None),
            P("wt"),
            P("wt"),
            P("wt", None),
            P("wt", None),
        ),
        check_vma=False,
    )
```

profile of v0, /device:TPU:0, one launch (start us, length us, event | category | flops | bytes accessed | tf_op | source)
XLA Modules:
  0.0 679.7 jit_solution(10840386280325061220)
XLA Ops:
  9.3 12.7 %all-gather = bf16[4,1,128]{2,1,0:T(2,128)(2,1)S(1)} all-gather(bf16[1,1,128]{2,1,0:T(2,128)(2,1)} %bitcast.256), channel_id=1, replica_groups=mesh['ctx'=8,'wt'=4] {'wt'}, dimensions={0}, use_global_device_ids=true | all-gather | bytes 1280 | tf_op jit(solution)/shard_map/all_gather | solution.py:52
  22.0 7.8 %all-gather.1 = bf16[4,1,128]{2,1,0:T(2,128)(2,1)S(1)} all-gather(bf16[1,1,128]{2,1,0:T(2,128)(2,1)} %bitcast.257), channel_id=1, replica_groups=mesh['ctx'=8,'wt'=4] {'wt'}, dimensions={0}, use_global_device_ids=true | all-gather | bytes 1280 | tf_op jit(solution)/shard_map/all_gather | solution.py:53
  32.0 18.6 %all-gather.9.cloned.1.call-done = bf16[512,1536]{0,1:T(8,128)(2,1)} async-done(((bf16[128,1536]{0,1:T(8,128)(2,1)}), bf16[512,1536]{0,1:T(8,128)(2,1)}) %all-gather.9.cloned.1.call-update) | async-done | bytes 1572880 | tf_op jit(solution)/shard_map/all_gather | solution.py:50
  53.6 4.4 reduce.16
  58.6 18.8 %all_to_all.40 = bf16[4,2,36864]{2,1,0:T(2,128)(2,1)S(1)} all-to-all(bf16[4,2,36864]{2,1,0:T(2,128)(2,1)S(1)} %reshape.330), channel_id=1, replica_groups=mesh['ctx'=8,'wt'=4] {'wt'}, dimensions={0} | all-to-all | bytes 1179648 | tf_op jit(solution)/shard_map/all_to_all | solution.py:65
  90.4 26.7 %all-gather.11.cloned.1.call-done = bf16[6144,256]{0,1:T(8,128)(2,1)} async-done(((bf16[768,256]{0,1:T(8,128)(2,1)}), bf16[6144,256]{0,1:T(8,128)(2,1)}) %all-gather.11.cloned.1.call-update) | async-done | bytes 3145744 | tf_op jit(solution)/shard_map/all_gather | solution.py:76
  122.3 84.7 %while.28 = (s32[]{:T(128)}, f32[2,768]{1,0:T(2,128)S(1)}, f32[2,768]{1,0:T(2,128)S(1)}, f32[768,2,64]{0,2,1:T(8,128)S(1)}, s32[8,768]{1,0:T(8,128)}, /*index=5*...) while((s32[]{:T(128)}, f32[2,768]{1,0:T(2,128)S(1)}, ...), condition=%wide.region_7.8_spmd.clone, body=%wide.region_4.7_spmd.clone.sunk | while | flops 317039616 | bytes 37675172 | solution.py:121
  213.4 4.5 all-to-all-start.1
  217.9 11.3 %all-gather.2 = bf16[4,1,128]{2,1,0:T(2,128)(2,1)S(1)} all-gather(bf16[1,1,128]{2,1,0:T(2,128)(2,1)S(1)} %bitcast.258), channel_id=1, replica_groups=mesh['ctx'=8,'wt'=4] {'wt'}, dimensions={0}, use_global_device_ids=true | all-gather | bytes 1280 | tf_op jit(solution)/shard_map/all_gather | solution.py:140
  229.2 7.7 %all-gather.3 = bf16[4,1,128]{2,1,0:T(2,128)(2,1)S(1)} all-gather(bf16[1,1,128]{2,1,0:T(2,128)(2,1)S(1)} %bitcast.259), channel_id=1, replica_groups=mesh['ctx'=8,'wt'=4] {'wt'}, dimensions={0}, use_global_device_ids=true | all-gather | bytes 1280 | tf_op jit(solution)/shard_map/all_gather | solution.py:141
  236.9 15.2 %all_gather.31 = bf16[512,512]{1,0:T(8,128)(2,1)S(1)} all-gather(bf16[128,512]{1,0:T(8,128)(2,1)S(1)} %copy-done.20), channel_id=1, replica_groups=mesh['ctx'=8,'wt'=4] {'wt'}, dimensions={0}, use_global_device_ids=true | all-gather | bytes 655360 | tf_op jit(solution)/shard_map/all_gather | solution.py:51
  254.2 6.9 %multiply_convert_fusion = (bf16[192,2048]{1,0:T(8,128)(2,1)}, f32[192,2048]{1,0:T(8,128)}, f32[192,2048]{1,0:T(8,128)}) fusion(bf16[512,2048]{1,0:T(8,128)(2,1)} %all-gather.13.cloned.1.call-done, f32[192,512]{1,0:T(8,128)S(1)} %get-tuple-element.400, f32[512]{0:T(512)S(1)} %bitcast.253, f32[512]{0:T(512)S(1)} %bitcast.249, f32[192]{0:T(256)S(1)} %add_rsqrt_fusion, ...), kind=kOutput, calls=%fused_computation.55 | convolution fusion | flops 428703744 | bytes 6428160 | tf_op jit(solution)/shard_map/dot_general | solution.py:147
  264.3 38.9 %all-reduce.4 = (f32[]{:T(128)}, f32[]{:T(128)}) all-reduce(f32[]{:T(128)} %get-tuple-element.324, f32[]{:T(128)} %get-tuple-element.323), channel_id=1, replica_groups=mesh['ctx'=8,'wt'=4] {'ctx','wt'}, use_global_device_ids=true, to_apply=%region_12.13 | all-reduce | flops 2 | bytes 16 | tf_op jit(solution)/shard_map/psum | solution.py:152
  318.0 5.9 all-to-all-done.2
  328.3 66.9 %while.29 = (s32[]{:T(128)}, f32[768,2,64]{0,2,1:T(8,128)S(1)}, bf16[8,768,2,2,64]{1,4,2,3,0:T(8,128)(2,1)}, bf16[8,768,2,2,64]{1,4,2,3,0:T(8,128)(2,1)}, s32[8,...) while((s32[]{:T(128)}, f32[768,2,64]{0,2,1:T(8,128)S(1)}, ...), condition=%wide.region_19.20_spmd.clone, body=%wide.region_18.19_spmd.clone.sunk | while | flops 769720320 | bytes 28011244 | solution.py:211
  409.4 38.5 %reduce-scatter.6.cloned.1.call-done = bf16[768,256]{0,1:T(8,128)(2,1)} async-done(((bf16[6144,256]{0,1:T(8,128)(2,1)}), bf16[768,256]{0,1:T(8,128)(2,1)}) %reduce-scatter.6.cloned.1.call-update) | async-done | bytes 393232 | tf_op jit(solution)/shard_map/reduce_scatter | solution.py:214
  452.1 5.6 reduce.19
  458.3 23.0 %all_to_all.41 = bf16[4,2,36864]{2,1,0:T(2,128)(2,1)S(1)} all-to-all(bf16[4,2,36864]{2,1,0:T(2,128)(2,1)S(1)} %reshape.336), channel_id=1, replica_groups=mesh['ctx'=8,'wt'=4] {'wt'}, dimensions={0} | all-to-all | bytes 1179648 | tf_op jit(solution)/shard_map/all_to_all | solution.py:223
  490.3 31.3 %reduce-scatter.12.cloned.1.call-done = bf16[128,2048]{1,0:T(8,128)(2,1)} async-done(((bf16[512,2048]{1,0:T(8,128)(2,1)}), bf16[128,2048]{1,0:T(8,128)(2,1)}) %reduce-scatter.12.cloned.1.call-update) | async-done | bytes 524304 | tf_op jit(solution)/shard_map/reduce_scatter | solution.py:259
  521.7 45.5 %reduce-scatter.14.cloned.1.call-done = bf16[512,512]{1,0:T(8,128)(2,1)} async-done(((bf16[2048,512]{1,0:T(8,128)(2,1)}), bf16[512,512]{1,0:T(8,128)(2,1)}) %reduce-scatter.14.cloned.1.call-update) | async-done | bytes 524304 | tf_op jit(solution)/shard_map/reduce_scatter | solution.py:262
  567.2 37.1 %reduce-scatter.8.cloned.1.call-done = bf16[128,1536]{1,0:T(8,128)(2,1)} async-done(((bf16[512,1536]{1,0:T(8,128)(2,1)}), bf16[128,1536]{1,0:T(8,128)(2,1)}) %reduce-scatter.8.cloned.1.call-update) | async-done | bytes 393232 | tf_op jit(solution)/shard_map/reduce_scatter | solution.py:247
  606.4 9.8 %all-reduce.7 = (bf16[512]{0:T(512)(128)(2,1)S(1)}, bf16[512]{0:T(512)(128)(2,1)S(1)}, bf16[512]{0:T(512)(128)(2,1)S(1)}, bf16[512]{0:T(512)(128)(2,1)S(1)}) all-reduce(bf16[512]{0:T(512)(128)(2,1)S(1)} %get-tuple-element.317, bf16[512]{0:T(512)(128)(2,1)S(1)} %get-tuple-element.322, ...), channel_id=3, replica_groups=mesh['ctx'=8,'wt'=4] {'wt'}, use_global_device_ids=true, to_apply=%region_24.25.clone | all-reduce | flops 2048 | bytes 8192
  616.5 11.9 %all-reduce.5 = (bf16[128]{0:T(256)(128)(2,1)S(1)}, bf16[128]{0:T(256)(128)(2,1)S(1)}, bf16[128]{0:T(256)(128)(2,1)S(1)}, bf16[128]{0:T(256)(128)(2,1)S(1)}) all-reduce(bf16[128]{0:T(256)(128)(2,1)S(1)} %dynamic-slice.1, bf16[128]{0:T(256)(128)(2,1)S(1)} %dynamic-slice.3, ...), channel_id=1, replica_groups=mesh['ctx'=8,'wt'=4] {'ctx'}, use_global_device_ids=true, to_apply=%region_25.26 | all-reduce | flops 512 | bytes 2048 | tf_op jit(solution)/shard_map/psum | solution.py:267
  631.3 35.2 %all-reduce.10.cloned.1.call-done = (bf16[128,1536]{1,0:T(8,128)(2,1)}, bf16[128,512]{1,0:T(8,128)(2,1)}, bf16[128,2048]{1,0:T(8,128)(2,1)}, bf16[512,512]{1,0:T(8,128)(2,1)}) async-done(((bf16[128,1536]{1,0:T(8,128)(2,1)}, bf16[128,512]{1,0:T(8,128)(2,1)}, bf16[128,2048]{1,0:T(8,128)(2,1)}, bf16[512,512]{1,0:T(8,128)(2,1)}), (bf16[128,1536]{1,0:T(8,128)(2,1)}, bf16[128,512]{1,0:T(8,128)(2,1)}, ...) | async-done | bytes 1572880 | tf_op jit(solution)/shard_map/psum | solution.py:269
  (426 shorter events, 243.0 us)
Async XLA Ops:
  7.2 43.5 %copy-start.3 = (bf16[192,512]{1,0:T(8,128)(2,1)S(1)}, bf16[192,512]{1,0:T(8,128)(2,1)}, u32[]{:S(2)}) copy-start(bf16[192,512]{1,0:T(8,128)(2,1)} %param.17) | copy-start | bytes 589828
  7.2 43.4 %all-gather.9.cloned.1.call-start = ((), (), s32[]{:S(2)}) async-start(), calls=%async_computation.9 | async-start | bytes 1966080 | tf_op jit(solution)/shard_map/all_gather | solution.py:50
  9.2 107.9 %all-gather.11.cloned.1.call-start = ((), (), s32[]{:S(2)}) async-start(), calls=%async_computation.10 | async-start | bytes 3538944 | tf_op jit(solution)/shard_map/all_gather | solution.py:76
  22.0 28.6 %copy-start.22 = (f32[4,1,128]{2,1,0:T(1,128)}, f32[4,1,128]{2,1,0:T(1,128)S(1)}, u32[]{:S(2)}) copy-start(f32[4,1,128]{2,1,0:T(1,128)S(1)} %convert_element_type.187) | copy-start | bytes 6148
  29.8 20.8 %copy-start.26 = (f32[4,1,128]{2,1,0:T(1,128)}, f32[4,1,128]{2,1,0:T(1,128)S(1)}, u32[]{:S(2)}) copy-start(f32[4,1,128]{2,1,0:T(1,128)S(1)} %convert_element_type.188) | copy-start | bytes 6148
  30.8 19.8 %copy-start.24 = (f32[192]{0:T(256)}, f32[192]{0:T(256)S(1)}, u32[]{:S(2)}) copy-start(f32[192]{0:T(256)S(1)} %broadcast_multiply_fusion.5) | copy-start | bytes 2308
  32.0 18.6 %copy-start.32 = (f32[192]{0:T(256)}, f32[192]{0:T(256)S(1)}, u32[]{:S(2)}) copy-start(f32[192]{0:T(256)S(1)} %add_rsqrt_fusion.1) | copy-start | bytes 2308
  85.4 168.8 %all-gather.13.cloned.1.call-start = ((), (), s32[]{:S(2)}) async-start(), calls=%async_computation.11 | async-start | bytes 2621440 | tf_op jit(solution)/shard_map/all_gather | solution.py:138
  86.1 175.0 %all-gather.15.cloned.1.call-start = ((), (), s32[]{:S(2)}) async-start(), calls=%async_computation.12 | async-start | bytes 2621440 | tf_op jit(solution)/shard_map/all_gather | solution.py:139
  210.4 18.9 %copy-start.44 = (bf16[128]{0:T(256)(128)(2,1)S(1)}, bf16[128]{0:T(256)(128)(2,1)}, u32[]{:S(2)}) copy-start(bf16[128]{0:T(256)(128)(2,1)} %param.27) | copy-start | bytes 772
  210.4 26.5 %copy-start.20 = (bf16[128,512]{1,0:T(8,128)(2,1)S(1)}, bf16[128,512]{1,0:T(8,128)(2,1)}, u32[]{:S(2)}) copy-start(bf16[128,512]{1,0:T(8,128)(2,1)} %param.25) | copy-start | bytes 393220
  213.4 38.7 %all-to-all-start.1 = ((bf16[4,2,12288]{2,1,0:T(2,128)(2,1)}), bf16[4,2,12288]{2,1,0:T(2,128)(2,1)S(1)}, u32[]{:S(2)}, u32[]{:S(2)}) async-start(bf16[4,2,12288]{2,1,0:T(2,128)(2,1)} %reshape.332), calls=%async_computation.1 | async-start | bytes 393216 | tf_op jit(solution)/shard_map/all_to_all | solution.py:127
  229.2 80.0 %copy-start.28 = (f32[4,1,128]{2,1,0:T(1,128)}, f32[4,1,128]{2,1,0:T(1,128)S(1)}, u32[]{:S(2)}) copy-start(f32[4,1,128]{2,1,0:T(1,128)S(1)} %convert_element_type.189) | copy-start | bytes 6148
  236.9 17.3 %copy-start.36 = (f32[4,1,128]{2,1,0:T(1,128)}, f32[4,1,128]{2,1,0:T(1,128)S(1)}, u32[]{:S(2)}) copy-start(f32[4,1,128]{2,1,0:T(1,128)S(1)} %convert_element_type.190) | copy-start | bytes 6148
  253.9 55.3 %copy-start.1 = (f32[192,512]{1,0:T(8,128)}, f32[192,512]{1,0:T(8,128)S(1)}, u32[]{:S(2)}) copy-start(f32[192,512]{1,0:T(8,128)S(1)} %get-tuple-element.400) | copy-start | bytes 1179652
  253.9 55.3 %copy-start.30 = (f32[192]{0:T(256)}, f32[192]{0:T(256)S(1)}, u32[]{:S(2)}) copy-start(f32[192]{0:T(256)S(1)} %broadcast_multiply_fusion.4) | copy-start | bytes 2308
  254.1 55.1 %copy-start.34 = (f32[192]{0:T(256)}, f32[192]{0:T(256)S(1)}, u32[]{:S(2)}) copy-start(f32[192]{0:T(256)S(1)} %add_rsqrt_fusion) | copy-start | bytes 2308
  313.3 10.5 %all-to-all-start.2 = ((bf16[4,2,12288]{2,1,0:T(2,128)(2,1)}), bf16[4,2,12288]{2,1,0:T(2,128)(2,1)S(1)}, u32[]{:S(2)}, u32[]{:S(2)}) async-start(bf16[4,2,12288]{2,1,0:T(2,128)(2,1)} %reshape.334), calls=%async_computation.2 | async-start | bytes 393216 | tf_op jit(solution)/shard_map/all_to_all | solution.py:176
  317.1 130.7 %reduce-scatter.6.cloned.1.call-start = ((), (), s32[]{:S(2)}) async-start(), calls=%async_computation.13 | async-start | bytes 3538944 | tf_op jit(solution)/shard_map/reduce_scatter | solution.py:214
  401.5 88.9 %reduce-scatter.10.cloned.1.call-start = ((), (), s32[]{:S(2)}) async-start(), calls=%async_computation.15 | async-start | bytes 655360 | tf_op jit(solution)/shard_map/reduce_scatter | solution.py:250
  403.6 118.1 %reduce-scatter.12.cloned.1.call-start = ((), (), s32[]{:S(2)}) async-start(), calls=%async_computation.16 | async-start | bytes 2621440 | tf_op jit(solution)/shard_map/reduce_scatter | solution.py:259
  405.9 161.3 %reduce-scatter.14.cloned.1.call-start = ((), (), s32[]{:S(2)}) async-start(), calls=%async_computation.17 | async-start | bytes 2621440 | tf_op jit(solution)/shard_map/reduce_scatter | solution.py:262
  409.3 195.0 %reduce-scatter.8.cloned.1.call-start = ((), (), s32[]{:S(2)}) async-start(), calls=%async_computation.14 | async-start | bytes 1966080 | tf_op jit(solution)/shard_map/reduce_scatter | solution.py:247
  488.4 178.2 %all-reduce.10.cloned.1.call-start = ((), (), s32[]{:S(2)}) async-start(), calls=%async_computation.18 | async-start | bytes 3145728 | tf_op jit(solution)/shard_map/psum | solution.py:269
  (65 other events, 152.8 us)
Sparse Core Ops, SparseCore 0:
  10.2 40.4 all-gather.8
  85.5 31.5 all-gather.10
  118.7 45.9 all-gather.12
  166.1 44.6 all-gather.14
  401.5 46.3 reduce-scatter.5
  450.7 23.8 reduce-scatter.9
  477.0 44.6 reduce-scatter.11
  523.9 43.1 reduce-scatter.13
  569.6 34.5 reduce-scatter.7
  608.1 58.3 all-reduce.9
where the time goes:
time: 687 us; the launch traced here: 680 us
  waiting for transfers between devices  240 us (35%)
  blocking collectives  157 us (23%)
  matrix products  124 us (18%)
  local copies, waits for them, and re-layouts  65.7 us (10%)
  other arithmetic  64.5 us (9%)
  between operations  18.4 us (3%)
  starting transfers between devices  9.25 us (1%)
    reduce_scatter x1, waiting for transfers between devices, per_device(): lax.psum_scatter(grad_down.astype(jnp.bfloat16), 'wt', scatter_dimension=...  45.5 us
    psum x1, blocking collectives, per_device(): lax.psum((jnp.sum(valid_float), jnp.sum(valid_float * jnp.sum(distance *...  38.9 us
    reduce_scatter x1, waiting for transfers between devices, per_device(): lax.psum_scatter(grad_pieces.reshape(ctx_count * group_rows, head_count *...  38.5 us
    reduce_scatter x1, waiting for transfers between devices, per_device(): lax.psum_scatter(grad_qkv.astype(jnp.bfloat16), 'wt', scatter_dimension=0...  37.1 us
    psum x1, waiting for transfers between devices, per_device(): lax.psum(shard_qkv.astype(jnp.bfloat16), 'ctx').astype(jnp.float32)  35.2 us
    dot_general x16, matrix products, scores_of(): jnp.einsum('qhd,khd->hqk', queries, kv_piece[:, :, 0], preferred_element_...  32 us
    reduce_scatter x1, waiting for transfers between devices, per_device(): lax.psum_scatter(grad_up.astype(jnp.bfloat16), 'wt', scatter_dimension=0,...  31.3 us
    dot_general x8, matrix products, forward_step(): jnp.einsum('hqk,khd->qhd', weights.astype(jnp.bfloat16), kv_piece[:, :, 1...  30.9 us
  transfers between devices with their start and end apart: 12, of which 8 were waited for; matrix products, arithmetic and copies ran while one was open for 20% of the time, Pallas kernels for 0%

commit v1 on v0

--- a/solution.py
+++ b/solution.py
@@ -263,10 +263,15 @@
             grad_down.astype(jnp.bfloat16), "wt", scatter_dimension=0, tiled=True
         ).astype(jnp.float32),
     )
+
+    def slices_set(slab_in, axis_key):
+        heard = jnp.sum(lax.all_gather(slab_in, axis_key), 0)
+        return heard
+
     summed = (
         lax.psum(shard_ga.astype(jnp.bfloat16), "ctx").astype(jnp.float32),
         lax.psum(shard_sa.astype(jnp.bfloat16), "ctx").astype(jnp.float32),
-        lax.psum(shard_qkv.astype(jnp.bfloat16), "ctx").astype(jnp.float32),
+        slices_set(shard_qkv.astype(jnp.bfloat16), "ctx").astype(jnp.float32),
         lax.psum(shard_out.astype(jnp.bfloat16), "ctx").astype(jnp.float32),
         lax.psum(shard_gm.astype(jnp.bfloat16), "ctx").astype(jnp.float32),
         lax.psum(shard_sm.astype(jnp.bfloat16), "ctx").astype(jnp.float32),

time: 687 us -> 709 us (1.032)
  matrix products: 124 us -> 88.4 us
  waiting for transfers between devices: 240 us -> 265 us
  other arithmetic: 64.5 us -> 80.1 us
  blocking collectives: 157 us -> 169 us
    psum x1, waiting for transfers between devices: 35.2 us -> 58.3 us  [per_device(): lax.psum(shard_out.astype(jnp.bfloat16), 'ctx').astype(jnp.float32)]
    dot_general x8, matrix products: 30.9 us -> 10.7 us  [forward_step(): jnp.einsum('hqk,khd->qhd', weights.astype(jnp.bfloat16), kv_piece[:, :, 1...]
    dot_general x16, matrix products: 32 us -> 15.2 us  [scores_of(): jnp.einsum('qhd,khd->hqk', queries, kv_piece[:, :, 0], preferred_element_...]
    squeeze x16, local copies, waits for them, and re-layouts: 16.5 us -> 0.56 us  [per_device(): lax.scan(forward_step, (start_max, start_sum, start_acc), scan_items)]
    unnamed x110 -> x106, local copies, waits for them, and re-layouts: 20.2 us -> 28.7 us
  transfers between devices with their start and end apart: 12 -> 13, of which waited for: 8 -> 9; matrix products, arithmetic and copies ran while one was open for 20% -> 15% of each run, Pallas kernels for 0% -> 0%
where the time goes in v1:
time: 709 us; the launch traced here: 701 us
  waiting for transfers between devices  265 us (37%)
  blocking collectives  169 us (24%)
  matrix products  88.4 us (12%)
  other arithmetic  80.1 us (11%)
  local copies, waits for them, and re-layouts  69.1 us (10%)
  between operations  18 us (3%)
  starting transfers between devices  9.64 us (1%)
    psum x1, waiting for transfers between devices, per_device(): lax.psum(shard_out.astype(jnp.bfloat16), 'ctx').astype(jnp.float32)  58.3 us
    reduce_scatter x1, waiting for transfers between devices, per_device(): lax.psum_scatter(grad_down.astype(jnp.bfloat16), 'wt', scatter_dimension=...  45.5 us
    psum x1, blocking collectives, per_device(): lax.psum((jnp.sum(valid_float), jnp.sum(valid_float * jnp.sum(distance *...  38.5 us
    reduce_scatter x1, waiting for transfers between devices, per_device(): lax.psum_scatter(grad_qkv.astype(jnp.bfloat16), 'wt', scatter_dimension=0...  37 us
    reduce_scatter x1, waiting for transfers between devices, per_device(): lax.psum_scatter(grad_pieces.reshape(ctx_count * group_rows, head_count *...  36.5 us
    reduce_scatter x1, waiting for transfers between devices, per_device(): lax.psum_scatter(grad_up.astype(jnp.bfloat16), 'wt', scatter_dimension=0,...  33.9 us
    unnamed x106, local copies, waits for them, and re-layouts  28.7 us
    all_gather x1, waiting for transfers between devices, per_device(): lax.all_gather(key_values, 'ctx', axis=0, tiled=True)  28 us
  transfers between devices with their start and end apart: 13, of which 9 were waited for; matrix products, arithmetic and copies ran while one was open for 15% of the time, Pallas kernels for 0%

profile of v1, /device:TPU:0, one launch (start us, length us, event | category | flops | bytes accessed | tf_op | source)
XLA Modules:
  0.0 701.3 jit_solution(15469828185903130465)
XLA Ops:
  9.3 12.7 %all-gather.1 = bf16[4,1,128]{2,1,0:T(2,128)(2,1)S(1)} all-gather(bf16[1,1,128]{2,1,0:T(2,128)(2,1)} %bitcast.258), channel_id=1, replica_groups=mesh['ctx'=8,'wt'=4] {'wt'}, dimensions={0}, use_global_device_ids=true | all-gather | bytes 1280 | tf_op jit(solution)/shard_map/all_gather | solution.py:52
  22.0 7.8 %all-gather.2 = bf16[4,1,128]{2,1,0:T(2,128)(2,1)S(1)} all-gather(bf16[1,1,128]{2,1,0:T(2,128)(2,1)} %bitcast.259), channel_id=1, replica_groups=mesh['ctx'=8,'wt'=4] {'wt'}, dimensions={0}, use_global_device_ids=true | all-gather | bytes 1280 | tf_op jit(solution)/shard_map/all_gather | solution.py:53
  32.0 18.6 %all-gather.11.cloned.1.call-done = bf16[512,1536]{0,1:T(8,128)(2,1)} async-done(((bf16[128,1536]{0,1:T(8,128)(2,1)}), bf16[512,1536]{0,1:T(8,128)(2,1)}) %all-gather.11.cloned.1.call-update) | async-done | bytes 1572880 | tf_op jit(solution)/shard_map/all_gather | solution.py:50
  53.6 4.4 reduce.17
  58.6 18.8 %all_to_all.40 = bf16[4,2,36864]{2,1,0:T(2,128)(2,1)S(1)} all-to-all(bf16[4,2,36864]{2,1,0:T(2,128)(2,1)S(1)} %reshape.331), channel_id=1, replica_groups=mesh['ctx'=8,'wt'=4] {'wt'}, dimensions={0} | all-to-all | bytes 1179648 | tf_op jit(solution)/shard_map/all_to_all | solution.py:65
  89.1 28.0 %all-gather.13.cloned.1.call-done = bf16[6144,256]{0,1:T(8,128)(2,1)} async-done(((bf16[768,256]{0,1:T(8,128)(2,1)}), bf16[6144,256]{0,1:T(8,128)(2,1)}) %all-gather.13.cloned.1.call-update) | async-done | bytes 3145744 | tf_op jit(solution)/shard_map/all_gather | solution.py:76
  120.6 44.8 %while.28 = (s32[]{:T(128)}, f32[2,768]{1,0:T(2,128)S(1)}, f32[2,768]{1,0:T(2,128)}, f32[768,2,64]{0,2,1:T(8,128)}, s32[8,768]{1,0:T(8,128)}, /*index=5*/s32[768...) while((s32[]{:T(128)}, f32[2,768]{1,0:T(2,128)S(1)}, ...), condition=%wide.region_7.8_spmd.clone, body=%wide.region_4.7_spmd.clone.sunk | while | flops 317039616 | bytes 21995776 | solution.py:121
  179.7 4.6 all-to-all-start.1
  184.3 13.2 %all-gather.3 = bf16[4,1,128]{2,1,0:T(2,128)(2,1)S(1)} all-gather(bf16[1,1,128]{2,1,0:T(2,128)(2,1)} %bitcast.260), channel_id=1, replica_groups=mesh['ctx'=8,'wt'=4] {'wt'}, dimensions={0}, use_global_device_ids=true | all-gather | bytes 1280 | tf_op jit(solution)/shard_map/all_gather | solution.py:140
  198.2 11.8 %all-gather.4 = bf16[4,1,128]{2,1,0:T(2,128)(2,1)S(1)} all-gather(bf16[1,1,128]{2,1,0:T(2,128)(2,1)} %bitcast.261), channel_id=1, replica_groups=mesh['ctx'=8,'wt'=4] {'wt'}, dimensions={0}, use_global_device_ids=true | all-gather | bytes 1280 | tf_op jit(solution)/shard_map/all_gather | solution.py:141
  210.5 17.1 %all_gather.37 = bf16[512,512]{1,0:T(8,128)(2,1)} all-gather(bf16[128,512]{1,0:T(8,128)(2,1)} %param.25), channel_id=1, replica_groups=mesh['ctx'=8,'wt'=4] {'wt'}, dimensions={0}, use_global_device_ids=true | all-gather | bytes 655360 | tf_op jit(solution)/shard_map/all_gather | solution.py:51
  235.7 7.3 %multiply_convert_fusion = (bf16[192,2048]{1,0:T(8,128)(2,1)}, f32[192,2048]{1,0:T(8,128)}, f32[192,2048]{1,0:T(8,128)}) fusion(bf16[512,2048]{1,0:T(8,128)(2,1)} %all-gather.15.cloned.1.call-done, f32[192,512]{1,0:T(8,128)} %copy-done.3, f32[512]{0:T(512)} %bitcast.255, f32[512]{0:T(512)} %bitcast.251, f32[192]{0:T(256)} %add_rsqrt_fusion, f32[192]{0:T(256)} %copy-done.35), kind=kOutput, calls=%fused_computation.55 | convolution fusion | flops 428703744 | bytes 6428160 | tf_op jit(solution)/shard_map/dot_general | solution.py:147
  246.9 38.5 %all-reduce.4 = (f32[]{:T(128)}, f32[]{:T(128)}) all-reduce(f32[]{:T(128)} %get-tuple-element.324, f32[]{:T(128)} %get-tuple-element.323), channel_id=1, replica_groups=mesh['ctx'=8,'wt'=4] {'ctx','wt'}, use_global_device_ids=true, to_apply=%region_12.13 | all-reduce | flops 2 | bytes 16 | tf_op jit(solution)/shard_map/psum | solution.py:152
  308.9 5.8 all-to-all-done.2
  328.4 59.1 %while.29 = (s32[]{:T(128)}, f32[768,2,64]{0,2,1:T(8,128)}, bf16[8,768,2,2,64]{1,4,2,3,0:T(8,128)(2,1)}, bf16[8,768,2,2,64]{1,4,2,3,0:T(8,128)(2,1)S(1)}, s32[8,...) while((s32[]{:T(128)}, f32[768,2,64]{0,2,1:T(8,128)}, ...), condition=%wide.region_19.20_spmd.clone, body=%wide.region_18.19_spmd.clone.sunk | while | flops 769720320 | bytes 31156524 | solution.py:211
  402.8 36.5 %reduce-scatter.6.cloned.1.call-done = bf16[768,256]{0,1:T(8,128)(2,1)} async-done(((bf16[6144,256]{0,1:T(8,128)(2,1)}), bf16[768,256]{0,1:T(8,128)(2,1)}) %reduce-scatter.6.cloned.1.call-update) | async-done | bytes 393232 | tf_op jit(solution)/shard_map/reduce_scatter | solution.py:214
  442.4 4.4 reduce.20
  447.5 25.3 %all_to_all.41 = bf16[4,2,36864]{2,1,0:T(2,128)(2,1)S(1)} all-to-all(bf16[4,2,36864]{2,1,0:T(2,128)(2,1)S(1)} %reshape.337), channel_id=1, replica_groups=mesh['ctx'=8,'wt'=4] {'wt'}, dimensions={0} | all-to-all | bytes 1179648 | tf_op jit(solution)/shard_map/all_to_all | solution.py:223
  479.8 33.9 %reduce-scatter.12.cloned.1.call-done = bf16[128,2048]{1,0:T(8,128)(2,1)} async-done(((bf16[512,2048]{1,0:T(8,128)(2,1)}), bf16[128,2048]{1,0:T(8,128)(2,1)}) %reduce-scatter.12.cloned.1.call-update) | async-done | bytes 524304 | tf_op jit(solution)/shard_map/reduce_scatter | solution.py:259
  513.7 45.5 %reduce-scatter.14.cloned.1.call-done = bf16[512,512]{1,0:T(8,128)(2,1)} async-done(((bf16[2048,512]{1,0:T(8,128)(2,1)}), bf16[512,512]{1,0:T(8,128)(2,1)}) %reduce-scatter.14.cloned.1.call-update) | async-done | bytes 524304 | tf_op jit(solution)/shard_map/reduce_scatter | solution.py:262
  559.2 37.0 %reduce-scatter.8.cloned.1.call-done = bf16[128,1536]{1,0:T(8,128)(2,1)} async-done(((bf16[512,1536]{1,0:T(8,128)(2,1)}), bf16[128,1536]{1,0:T(8,128)(2,1)}) %reduce-scatter.8.cloned.1.call-update) | async-done | bytes 393232 | tf_op jit(solution)/shard_map/reduce_scatter | solution.py:247
  598.2 58.3 %all-reduce.10.cloned.1.call-done = (bf16[128,512]{1,0:T(8,128)(2,1)}, bf16[128,2048]{1,0:T(8,128)(2,1)}, bf16[512,512]{1,0:T(8,128)(2,1)}) async-done(((bf16[128,512]{1,0:T(8,128)(2,1)}, bf16[128,2048]{1,0:T(8,128)(2,1)}, bf16[512,512]{1,0:T(8,128)(2,1)}), (bf16[128,512]{1,0:T(8,128)(2,1)}, bf16[128,2048]{1,0:T(8,128)(2,1)}, bf16[512,512]{1,0:T(8,128)(2,1)})) %all-reduce.10.cloned.1.call-update) | async-done | bytes 1179664 | tf_op jit(solution)/shard_map/psum | solution.py:275
  662.2 11.7 %all-reduce.7 = (bf16[512]{0:T(512)(128)(2,1)S(1)}, bf16[512]{0:T(512)(128)(2,1)S(1)}, bf16[512]{0:T(512)(128)(2,1)S(1)}, bf16[512]{0:T(512)(128)(2,1)S(1)}) all-reduce(bf16[512]{0:T(512)(128)(2,1)S(1)} %get-tuple-element.317, bf16[512]{0:T(512)(128)(2,1)S(1)} %get-tuple-element.322, ...), channel_id=4, replica_groups=mesh['ctx'=8,'wt'=4] {'wt'}, use_global_device_ids=true, to_apply=%region_24.25.clone | all-reduce | flops 2048 | bytes 8192
  674.2 12.1 %all-reduce.5 = (bf16[128]{0:T(256)(128)(2,1)S(1)}, bf16[128]{0:T(256)(128)(2,1)S(1)}, bf16[128]{0:T(256)(128)(2,1)S(1)}, bf16[128]{0:T(256)(128)(2,1)S(1)}) all-reduce(bf16[128]{0:T(256)(128)(2,1)S(1)} %dynamic-slice.1, bf16[128]{0:T(256)(128)(2,1)S(1)} %dynamic-slice.3, ...), channel_id=1, replica_groups=mesh['ctx'=8,'wt'=4] {'ctx'}, use_global_device_ids=true, to_apply=%region_25.26 | all-reduce | flops 512 | bytes 2048 | tf_op jit(solution)/shard_map/psum | solution.py:272
  (506 shorter events, 228.3 us)
Async XLA Ops:
  7.2 43.5 %copy-start.6 = (bf16[192,512]{1,0:T(8,128)(2,1)S(1)}, bf16[192,512]{1,0:T(8,128)(2,1)}, u32[]{:S(2)}) copy-start(bf16[192,512]{1,0:T(8,128)(2,1)} %param.17) | copy-start | bytes 589828
  7.2 43.4 %all-gather.11.cloned.1.call-start = ((), (), s32[]{:S(2)}) async-start(), calls=%async_computation.9 | async-start | bytes 1966080 | tf_op jit(solution)/shard_map/all_gather | solution.py:50
  9.2 107.9 %all-gather.13.cloned.1.call-start = ((), (), s32[]{:S(2)}) async-start(), calls=%async_computation.10 | async-start | bytes 3538944 | tf_op jit(solution)/shard_map/all_gather | solution.py:76
  22.0 28.6 %copy-start.27 = (f32[4,1,128]{2,1,0:T(1,128)}, f32[4,1,128]{2,1,0:T(1,128)S(1)}, u32[]{:S(2)}) copy-start(f32[4,1,128]{2,1,0:T(1,128)S(1)} %convert_element_type.189) | copy-start | bytes 6148
  29.8 20.8 %copy-start.31 = (f32[4,1,128]{2,1,0:T(1,128)}, f32[4,1,128]{2,1,0:T(1,128)S(1)}, u32[]{:S(2)}) copy-start(f32[4,1,128]{2,1,0:T(1,128)S(1)} %convert_element_type.190) | copy-start | bytes 6148
  30.8 19.8 %copy-start.29 = (f32[192]{0:T(256)}, f32[192]{0:T(256)S(1)}, u32[]{:S(2)}) copy-start(f32[192]{0:T(256)S(1)} %broadcast_multiply_fusion.5) | copy-start | bytes 2308
  32.0 18.6 %copy-start.38 = (f32[192]{0:T(256)}, f32[192]{0:T(256)S(1)}, u32[]{:S(2)}) copy-start(f32[192]{0:T(256)S(1)} %add_rsqrt_fusion.1) | copy-start | bytes 2308
  85.4 150.3 %all-gather.15.cloned.1.call-start = ((), (), s32[]{:S(2)}) async-start(), calls=%async_computation.11 | async-start | bytes 2621440 | tf_op jit(solution)/shard_map/all_gather | solution.py:138
  86.1 156.9 %all-gather.17.cloned.1.call-start = ((), (), s32[]{:S(2)}) async-start(), calls=%async_computation.12 | async-start | bytes 2621440 | tf_op jit(solution)/shard_map/all_gather | solution.py:139
  179.7 47.9 %all-to-all-start.1 = ((bf16[4,2,12288]{2,1,0:T(2,128)(2,1)}), bf16[4,2,12288]{2,1,0:T(2,128)(2,1)}, u32[]{:S(2)}, u32[]{:S(2)}) async-start(bf16[4,2,12288]{2,1,0:T(2,128)(2,1)} %reshape.333), calls=%async_computation.1 | async-start | bytes 393216 | tf_op jit(solution)/shard_map/all_to_all | solution.py:127
  288.0 3.8 copy-start.15
  288.0 3.8 copy-start.4
  288.0 3.8 copy-start.33
  288.0 3.8 copy-start.36
  303.4 11.4 %all-to-all-start.2 = ((bf16[4,2,12288]{2,1,0:T(2,128)(2,1)}), bf16[4,2,12288]{2,1,0:T(2,128)(2,1)}, u32[]{:S(2)}, u32[]{:S(2)}) async-start(bf16[4,2,12288]{2,1,0:T(2,128)(2,1)} %reshape.335), calls=%async_computation.2 | async-start | bytes 393216 | tf_op jit(solution)/shard_map/all_to_all | solution.py:176
  307.4 131.9 %reduce-scatter.6.cloned.1.call-start = ((), (), s32[]{:S(2)}) async-start(), calls=%async_computation.13 | async-start | bytes 3538944 | tf_op jit(solution)/shard_map/reduce_scatter | solution.py:214
  393.8 86.0 %reduce-scatter.10.cloned.1.call-start = ((), (), s32[]{:S(2)}) async-start(), calls=%async_computation.15 | async-start | bytes 655360 | tf_op jit(solution)/shard_map/reduce_scatter | solution.py:250
  395.9 117.7 %reduce-scatter.12.cloned.1.call-start = ((), (), s32[]{:S(2)}) async-start(), calls=%async_computation.16 | async-start | bytes 2621440 | tf_op jit(solution)/shard_map/reduce_scatter | solution.py:259
  398.5 160.7 %reduce-scatter.14.cloned.1.call-start = ((), (), s32[]{:S(2)}) async-start(), calls=%async_computation.17 | async-start | bytes 2621440 | tf_op jit(solution)/shard_map/reduce_scatter | solution.py:262
  401.8 194.5 %reduce-scatter.8.cloned.1.call-start = ((), (), s32[]{:S(2)}) async-start(), calls=%async_computation.14 | async-start | bytes 1966080 | tf_op jit(solution)/shard_map/reduce_scatter | solution.py:247
  479.7 116.6 %copy-start.51 = (u32[32]{0:T(128)S(1)}, u32[32]{0:T(128)}, u32[]{:S(2)}) copy-start(u32[32]{0:T(128)} %constant.143) | copy-start | bytes 388
  479.7 176.7 %all-reduce.10.cloned.1.call-start = ((), (), s32[]{:S(2)}) async-start(), calls=%async_computation.19 | async-start | bytes 2359296 | tf_op jit(solution)/shard_map/psum | solution.py:275
  559.2 130.8 %all-gather.19.cloned.1.call-start = ((), (), s32[]{:S(2)}) async-start(), calls=%async_computation.18 | async-start | bytes 3538944 | tf_op jit(solution)/shard_map/all_gather | solution.py:268
  656.4 3.9 copy-start.19
  (104 other events, 136.5 us)
Sparse Core Ops, SparseCore 0:
  10.2 40.4 all-gather.10
  85.5 31.5 all-gather.12
  118.7 46.2 all-gather.14
  166.3 50.5 all-gather.16
  393.9 45.3 reduce-scatter.5
  442.1 24.5 reduce-scatter.9
  469.1 44.5 reduce-scatter.11
  516.0 43.1 reduce-scatter.13
  561.6 34.5 reduce-scatter.7
  600.0 56.4 all-reduce.9
  658.3 31.6 all-gather.18
